TPU v7x, 32 devices: a whole 2x2x4 slice. The times are simulated.
32 devices in a mesh: dp: 8 (over y, x, core), expert: 4 (over z).
Axes of the slice: x: 2, y: 2, z: 4, core: 2. Of those that a mesh axis runs over, the one named last changes fastest.
Arguments:
- tokens: bfloat16 [4096, 2048], P(('dp', 'expert')), may hold values from -6 to 6
- w_qkv: bfloat16 [3, 2048, 2048], P(None, 'dp', 'expert'), may hold values from -0.125 to 0.125
- w_out: bfloat16 [2048, 2048], P('expert', 'dp'), may hold values from -0.5 to 0.5
- attention_norm_gain: bfloat16 [2048], P('dp'), may hold values from 0.5 to 1.5
- gain_ffn: bfloat16 [2048], P('dp'), may hold values from 0.5 to 1.5
- w_router: bfloat16 [2048, 4], P('dp'), may hold values from -0.09375 to 0.09375
- w_gate_up: bfloat16 [4, 2048, 11264], P('expert', 'dp'), may hold values from -0.125 to 0.125
- w_down: bfloat16 [4, 5632, 2048], P('expert', 'dp'), may hold values from -0.15625 to 0.15625
- lengths: int32 [8], P('dp'), may hold values from 128 to 512, as said below
- routes: int32 [4096, 2], P(('dp', 'expert')), may hold values from 0 to 3, all different within a row
- order: int32 [4096], P(('dp', 'expert')), may hold values from 0 to 127, as said below
- cotangent: bfloat16 [4096, 2048], P(('dp', 'expert')), may hold values from -6 to 6
Outputs:
- output: bfloat16 [4096, 2048], P(('dp', 'expert'))
- grad_tokens: bfloat16 [4096, 2048], P(('dp', 'expert'))
- grad_qkv: float32 [3, 2048, 2048], P(None, 'dp', 'expert')
- grad_out: float32 [2048, 2048], P('expert', 'dp')
- grad_gain_attn: float32 [2048], P('dp')
- grad_gain_ffn: float32 [2048], P('dp')
- grad_router: float32 [2048, 4], P('dp')
- grad_gate_up: float32 [4, 2048, 11264], P('expert', 'dp')
- grad_down: float32 [4, 5632, 2048], P('expert', 'dp')
Inputs may be any that keep to these rules, and one draw needn't show every extreme that they name: `lengths`: one sequence of every draw has exactly 512 live tokens. `routes`: each token slot names 2 different experts, and every expert is named somewhere. `order`: each aligned block of 128 entries holds every number of 0 to 127 once.
All inputs are finite; a program needn't handle non-finite values.
Results may differ from a plain program's by a relative error of at most 0.023.
Values may be sent and summed in bfloat16 or wider, within the bound.
A program may use at most 384 MiB of HBM per device.

v0:
```python
import jax
import jax.numpy as jnp
from jax import lax
from jax.sharding import PartitionSpec as P

HEAD_DIM = 128
FF = 5632
NORM_EPSILON = 1e-05
NEGATIVE = -1e30
THETA = 10000.0
HIGH = lax.Precision.HIGHEST


def rotary_tables(length_total, head_size):
    position = jnp.arange(length_total, dtype=jnp.float32)
    frequency = THETA ** (-(jnp.arange(head_size // 2, dtype=jnp.float32) * 2.0 / head_size))
    angles = position[:, None] * frequency[None, :]
    return (jnp.cos(angles)[:, None, :], jnp.sin(angles)[:, None, :])


def rotate(values, cosine, sine):
    half_size = values.shape[-1] // 2
    first = values[..., :half_size]
    second = values[..., half_size:]
    return jnp.concatenate(
        [first * cosine - second * sine, second * cosine + first * sine], axis=-1
    )


def rotate_back(grad_rows, cosine, sine):
    half_size = grad_rows.shape[-1] // 2
    first = grad_rows[..., :half_size]
    second = grad_rows[..., half_size:]
    return jnp.concatenate(
        [first * cosine + second * sine, second * cosine - first * sine], axis=-1
    )


def slot_table(routes, order, valid, capacity):
    row_count = routes.shape[0]
    top_count = routes.shape[1]
    pair_rank = order[:, None] + row_count * jnp.arange(top_count, dtype=jnp.int32)[None, :]
    flat_rank = pair_rank.reshape(-1)
    flat_expert = routes.reshape(-1)
    flat_valid = jnp.broadcast_to(valid[:, None], routes.shape).reshape(-1)
    earlier = (
        (flat_rank[None, :] < flat_rank[:, None])
        & (flat_expert[None, :] == flat_expert[:, None])
        & flat_valid[None, :]
    )
    slot_index = jnp.sum(earlier.astype(jnp.int32), axis=1).reshape(row_count, top_count)
    kept_pair = valid[:, None] & (slot_index < capacity)
    target = routes * capacity + jnp.minimum(slot_index, capacity - 1)
    return (target, kept_pair)


def masked_scores(query, key_rows, allowed):
    scale = query.shape[-1] ** (-0.5)
    raw = jnp.einsum("qhd,khd->hqk", query, key_rows, preferred_element_type=jnp.float32) * scale
    return jnp.where(allowed[None], raw, NEGATIVE)


def fetch_expert(w_gate_up, w_down):
    gate_up_full, down_full = (
        lax.all_gather(w_gate_up, "dp", axis=1, tiled=True),
        lax.all_gather(w_down, "dp", axis=1, tiled=True),
    )
    return (gate_up_full[0], down_full[0])


def contract_first(left, right):
    return lax.dot_general(
        left, right, (((0,), (0,)), ((), ())), preferred_element_type=jnp.float32
    )


def contract_last(left, right):
    return lax.dot_general(
        left, right, (((1,), (1,)), ((), ())), preferred_element_type=jnp.float32
    )


def on_device(
    tokens,
    w_qkv,
    w_out,
    attention_norm_gain,
    gain_ffn,
    w_router,
    w_gate_up,
    w_down,
    lengths,
    routes,
    order,
    cotangent,
):
    group_size = lax.axis_size("expert")
    tok_dev = tokens.shape[0]
    seq_len = tok_dev * group_size
    width = tokens.shape[1]
    top_count = routes.shape[1]
    capacity = tok_dev * top_count // group_size
    head_size = HEAD_DIM
    local_width = w_qkv.shape[2]
    heads_local = local_width // head_size
    ff_width = FF
    qkv_full, out_full, first_norm_gain, gain_two, router_full = (
        lax.all_gather(w_qkv, "dp", axis=1, tiled=True),
        lax.all_gather(w_out, "dp", axis=1, tiled=True),
        lax.all_gather(attention_norm_gain, "dp", axis=0, tiled=True),
        lax.all_gather(gain_ffn, "dp", axis=0, tiled=True),
        lax.all_gather(w_router, "dp", axis=0, tiled=True),
    )
    first_norm_gain = first_norm_gain.astype(jnp.float32)
    gain_two = gain_two.astype(jnp.float32)
    own_start = lax.axis_index("expert") * tok_dev
    own_position = own_start + jnp.arange(tok_dev, dtype=jnp.int32)
    live_own = own_position < lengths[0]
    live_rows = live_own.astype(jnp.float32)[:, None]
    inputs_float = tokens.astype(jnp.float32)
    first_inverse_rms = lax.rsqrt(
        jnp.mean(inputs_float * inputs_float, axis=-1, keepdims=True) + NORM_EPSILON
    )
    input_normalized_hat = inputs_float * first_inverse_rms
    normalized_input = (input_normalized_hat * first_norm_gain).astype(jnp.bfloat16)
    whole = lax.all_gather(normalized_input, "expert", axis=0, tiled=True)
    cosine, sine = rotary_tables(seq_len, head_size)
    projected = jnp.einsum("td,cde->cte", whole, qkv_full, preferred_element_type=jnp.float32)
    query = rotate(projected[0].reshape(seq_len, heads_local, head_size), cosine, sine).astype(
        jnp.bfloat16
    )
    key_rows = rotate(projected[1].reshape(seq_len, heads_local, head_size), cosine, sine).astype(
        jnp.bfloat16
    )
    value = projected[2].astype(jnp.bfloat16).reshape(seq_len, heads_local, head_size)
    position = jnp.arange(seq_len, dtype=jnp.int32)
    live_all = position < lengths[0]
    allowed = (position[None, :] <= position[:, None]) & live_all[None, :]
    scores = masked_scores(query, key_rows, allowed)
    top_score = jnp.max(scores, axis=-1, keepdims=True)
    exponent = jnp.exp(scores - top_score)
    row_total = jnp.sum(exponent, axis=-1, keepdims=True)
    probs = exponent / row_total
    log_total = top_score + jnp.log(row_total)
    probs_low = probs.astype(jnp.bfloat16)
    attended = jnp.einsum("hqk,khd->qhd", probs_low, value, preferred_element_type=jnp.float32)
    attended = attended.reshape(seq_len, local_width).astype(jnp.bfloat16)
    attn_part = jnp.dot(attended, out_full, preferred_element_type=jnp.float32)
    attn_own = lax.psum_scatter(
        attn_part.astype(jnp.bfloat16), "expert", scatter_dimension=0, tiled=True
    ).astype(jnp.float32)
    resid = inputs_float + attn_own
    inverse_two = lax.rsqrt(jnp.mean(resid * resid, axis=-1, keepdims=True) + NORM_EPSILON)
    hhat = resid * inverse_two
    hidden_in = (hhat * gain_two).astype(jnp.bfloat16)
    logits = jnp.dot(hidden_in, router_full, preferred_element_type=jnp.float32)
    chosen = jnp.take_along_axis(logits, routes, axis=1)
    gates = jax.nn.softmax(chosen, axis=1)
    target, kept_pair = slot_table(routes, order, live_own, capacity)
    slot_ids = jnp.arange(group_size * capacity, dtype=jnp.int32)
    pair_hits = (slot_ids[:, None, None] == target[None]) & kept_pair[None]
    select = jnp.sum(pair_hits.astype(jnp.float32), axis=2).astype(jnp.bfloat16)
    sent = jnp.dot(select, hidden_in, preferred_element_type=jnp.float32).astype(jnp.bfloat16)
    received = lax.all_to_all(
        sent.reshape(group_size, capacity, width), "expert", split_axis=0, concat_axis=0, tiled=True
    )
    dispatched = received.reshape(group_size * capacity, width)
    gate_up_full, down_full = fetch_expert(w_gate_up, w_down)
    gate_up = jnp.dot(dispatched, gate_up_full, preferred_element_type=jnp.float32)
    gate = gate_up[:, :ff_width]
    upward = gate_up[:, ff_width:]
    sigmoid = jax.nn.sigmoid(gate)
    activated = (gate * sigmoid * upward).astype(jnp.bfloat16)
    expert_out = jnp.dot(activated, down_full, preferred_element_type=jnp.float32).astype(
        jnp.bfloat16
    )
    returned = lax.all_to_all(
        expert_out.reshape(group_size, capacity, width),
        "expert",
        split_axis=0,
        concat_axis=0,
        tiled=True,
    )
    returned = returned.reshape(group_size * capacity, width)
    moe = jnp.zeros_like(resid)
    picked_rows = []
    for index in range(top_count):
        one_hot = pair_hits[:, :, index].astype(jnp.bfloat16)
        picked = contract_first(one_hot, returned)
        picked_rows.append(picked)
        moe = moe + gates[:, index : index + 1] * picked
    output = (live_rows * (resid + moe)).astype(jnp.bfloat16)
    d_out = live_rows * cotangent.astype(jnp.float32)
    d_gates_list = []
    d_back = jnp.zeros((group_size * capacity, width), jnp.float32)
    for index in range(top_count):
        d_gates_list.append(jnp.sum(d_out * picked_rows[index], axis=-1))
        weighted = (gates[:, index : index + 1] * d_out).astype(jnp.bfloat16)
        d_back = d_back + jnp.dot(
            pair_hits[:, :, index].astype(jnp.bfloat16),
            weighted,
            preferred_element_type=jnp.float32,
        )
    d_gates = jnp.stack(d_gates_list, axis=1)
    d_back = d_back.astype(jnp.bfloat16)
    d_out_rows = lax.all_to_all(
        d_back.reshape(group_size, capacity, width),
        "expert",
        split_axis=0,
        concat_axis=0,
        tiled=True,
    )
    d_out_rows = d_out_rows.reshape(group_size * capacity, width)
    gate_up_back, down_back = fetch_expert(w_gate_up, w_down)
    d_activated = contract_last(d_out_rows, down_back)
    columns = activated
    grad_down = lax.psum_scatter(
        contract_first(columns, d_out_rows), "dp", scatter_dimension=0, tiled=True
    )
    silu_gate = gate * sigmoid
    d_gate = d_activated * upward * sigmoid * (1.0 + gate * (1.0 - sigmoid))
    d_up = d_activated * silu_gate
    d_gate_up = jnp.concatenate([d_gate, d_up], axis=1).astype(jnp.bfloat16)
    columns = dispatched
    grad_gate_up = lax.psum_scatter(
        contract_first(columns, d_gate_up), "dp", scatter_dimension=0, tiled=True
    )
    d_rows = contract_last(d_gate_up, gate_up_back).astype(jnp.bfloat16)
    d_sent = lax.all_to_all(
        d_rows.reshape(group_size, capacity, width),
        "expert",
        split_axis=0,
        concat_axis=0,
        tiled=True,
    )
    d_hidden = contract_first(select, d_sent.reshape(group_size * capacity, width))
    d_chosen = gates * (d_gates - jnp.sum(gates * d_gates, axis=1, keepdims=True))
    expert_ids = jnp.arange(group_size, dtype=jnp.int32)
    route_hits = (routes[:, :, None] == expert_ids[None, None, :]).astype(jnp.float32)
    d_logits = jnp.sum(route_hits * d_chosen[:, :, None], axis=1)
    router_f = router_full.astype(jnp.float32)
    d_hidden = d_hidden + jnp.dot(
        d_logits, router_f.T, precision=HIGH, preferred_element_type=jnp.float32
    )
    router_part = jnp.dot(
        hidden_in.astype(jnp.float32).T,
        d_logits,
        precision=HIGH,
        preferred_element_type=jnp.float32,
    )
    gain_two_part = jnp.sum(d_hidden * hhat, axis=0)
    scaled_two = d_hidden * gain_two
    d_resid = d_out + inverse_two * (
        scaled_two - hhat * jnp.mean(scaled_two * hhat, axis=-1, keepdims=True)
    )
    d_attn = d_resid.astype(jnp.bfloat16)
    whole_grad = lax.all_gather(d_attn, "expert", axis=0, tiled=True)
    out_part = contract_first(attended, whole_grad)
    d_attended = contract_last(whole_grad, out_full).astype(jnp.bfloat16)
    d_heads = d_attended.reshape(seq_len, heads_local, head_size)
    probs = jnp.exp(masked_scores(query, key_rows, allowed) - log_total)
    probs_low = probs.astype(jnp.bfloat16)
    d_value = jnp.einsum(
        "hqk,qhd->khd", probs_low, d_heads, preferred_element_type=jnp.float32
    ).astype(jnp.bfloat16)
    d_probs = jnp.einsum("qhd,khd->hqk", d_heads, value, preferred_element_type=jnp.float32)
    row_delta = jnp.sum(probs * d_probs, axis=-1, keepdims=True)
    d_scores = (probs * (d_probs - row_delta)).astype(jnp.bfloat16)
    scale = head_size ** (-0.5)
    d_query = (
        jnp.einsum("hqk,khd->qhd", d_scores, key_rows, preferred_element_type=jnp.float32) * scale
    )
    d_key = jnp.einsum("hqk,qhd->khd", d_scores, query, preferred_element_type=jnp.float32) * scale
    d_query_pre = (
        rotate_back(d_query, cosine, sine).reshape(seq_len, local_width).astype(jnp.bfloat16)
    )
    d_key_pre = rotate_back(d_key, cosine, sine).reshape(seq_len, local_width).astype(jnp.bfloat16)
    d_projected = jnp.stack([d_query_pre, d_key_pre, d_value.reshape(seq_len, local_width)])
    qkv_part = jnp.einsum("td,cte->cde", whole, d_projected, preferred_element_type=jnp.float32)
    d_normed_part = jnp.einsum(
        "cte,cde->td", d_projected, qkv_full, preferred_element_type=jnp.float32
    )
    grad_normalized = lax.psum_scatter(
        d_normed_part.astype(jnp.bfloat16), "expert", scatter_dimension=0, tiled=True
    ).astype(jnp.float32)
    first_gain_piece = jnp.sum(grad_normalized * input_normalized_hat, axis=0)
    first_scaled_input = grad_normalized * first_norm_gain
    grad_tokens = d_resid + first_inverse_rms * (
        first_scaled_input
        - input_normalized_hat
        * jnp.mean(first_scaled_input * input_normalized_hat, axis=-1, keepdims=True)
    )
    gain_one_sum, gain_two_sum, router_sum = (
        lax.psum(first_gain_piece.astype(jnp.bfloat16), "expert").astype(jnp.float32),
        lax.psum(gain_two_part.astype(jnp.bfloat16), "expert").astype(jnp.float32),
        lax.psum(router_part.astype(jnp.bfloat16), "expert").astype(jnp.float32),
    )
    grad_qkv, grad_out, grad_gain_attn, grad_gain_ffn, grad_router = (
        lax.psum_scatter(qkv_part, "dp", scatter_dimension=1, tiled=True),
        lax.psum_scatter(out_part, "dp", scatter_dimension=1, tiled=True),
        lax.psum_scatter(gain_one_sum, "dp", scatter_dimension=0, tiled=True),
        lax.psum_scatter(gain_two_sum, "dp", scatter_dimension=0, tiled=True),
        lax.psum_scatter(router_sum, "dp", scatter_dimension=0, tiled=True),
    )
    return (
        output,
        grad_tokens.astype(jnp.bfloat16),
        grad_qkv,
        grad_out,
        grad_gain_attn,
        grad_gain_ffn,
        grad_router,
        grad_gate_up[None],
        grad_down[None],
    )


def solution(mesh):
    placed = (
        P(("dp", "expert"), None),
        P(None, "dp", "expert"),
        P("expert", "dp"),
        P("dp"),
        P("dp"),
        P("dp", None),
        P("expert", "dp", None),
        P("expert", "dp", None),
        P("dp"),
        P(("dp", "expert"), None),
        P(("dp", "expert")),
        P(("dp", "expert"), None),
    )
    return jax.shard_map(
        on_device,
        mesh=mesh,
        in_specs=placed,
        out_specs=(
            P(("dp", "expert"), None),
            P(("dp", "expert"), None),
            P(None, "dp", "expert"),
            P("expert", "dp"),
            P("dp"),
            P("dp"),
            P("dp", None),
            P("expert", "dp", None),
            P("expert", "dp", None),
        ),
        check_vma=False,
    )
```

profile of v0, /device:TPU:0, one launch (start us, length us, event | category | flops | bytes accessed | tf_op | source)
XLA Modules:
  0.0 1797.1 jit_solution(4819094658459941075)
XLA Ops:
  9.1 10.3 all-gather
  27.9 40.1 %all-gather.9.cloned.1.call-done = bf16[512,2048]{1,0:T(8,128)(2,1)} async-done(((bf16[128,2048]{1,0:T(8,128)(2,1)}), bf16[512,2048]{1,0:T(8,128)(2,1)}) %all-gather.9.cloned.1.call-update) | async-done | bytes 2097168 | tf_op jit(solution)/shard_map/all_gather | solution.py:126
  67.9 47.9 %all-gather.11.cloned.1.call-done = bf16[3,2048,512]{1,2,0:T(8,128)(2,1)} async-done(((bf16[3,256,512]{1,2,0:T(8,128)(2,1)}), bf16[3,2048,512]{1,2,0:T(8,128)(2,1)}) %all-gather.11.cloned.1.call-update) | async-done | bytes 6291472 | tf_op jit(solution)/shard_map/all_gather | solution.py:108
  162.4 31.7 %reduce-scatter.12.cloned.1.call-done = bf16[128,2048]{1,0:T(8,128)(2,1)} async-done(((bf16[512,2048]{1,0:T(8,128)(2,1)}), bf16[128,2048]{1,0:T(8,128)(2,1)}) %reduce-scatter.12.cloned.1.call-update) | async-done | bytes 524304 | tf_op jit(solution)/shard_map/reduce_scatter | solution.py:149
  197.2 28.8 %all_to_all.20 = bf16[4,64,2048]{2,1,0:T(8,128)(2,1)S(1)} all-to-all(bf16[4,64,2048]{2,1,0:T(8,128)(2,1)S(1)} %bitcast.116), channel_id=1, replica_groups=mesh['dp'=8,'expert'=4] {'expert'}, dimensions={0} | all-to-all | bytes 2097152 | tf_op jit(solution)/shard_map/all_to_all | solution.py:164
  226.0 184.1 %all-gather.15.cloned.1.call-done = bf16[1,2048,11264]{2,1,0:T(8,128)(2,1)} async-done(((bf16[1,256,11264]{2,1,0:T(8,128)(2,1)}), bf16[1,2048,11264]{2,1,0:T(8,128)(2,1)}) %all-gather.15.cloned.1.call-update) | async-done | bytes 46137360 | tf_op jit(solution)/shard_map/all_gather | solution.py:65
  410.1 25.9 %fusion.2 = f32[256,11264]{1,0:T(8,128)} fusion(bf16[256,2048]{1,0:T(8,128)(2,1)S(1)} %bitcast.114, bf16[1,2048,11264]{2,1,0:T(8,128)(2,1)} %all-gather.15.cloned.1.call-done), kind=kOutput, calls=%fused_computation.3 | convolution fusion | flops 11811160064 | bytes 58720256 | tf_op jit(solution)/shard_map/dot_general | solution.py:169
  441.2 87.4 %all-gather.17.cloned.1.call-done = bf16[1,5632,2048]{2,1,0:T(8,128)(2,1)} async-done(((bf16[1,704,2048]{2,1,0:T(8,128)(2,1)}), bf16[1,5632,2048]{2,1,0:T(8,128)(2,1)}) %all-gather.17.cloned.1.call-update) | async-done | bytes 23068688 | tf_op jit(solution)/shard_map/all_gather | solution.py:66
  528.5 12.0 fusion.12
  579.3 27.9 %all_to_all.21 = bf16[4,64,2048]{2,1,0:T(8,128)(2,1)S(1)} all-to-all(bf16[4,64,2048]{2,1,0:T(8,128)(2,1)S(1)} %bitcast.119), channel_id=1, replica_groups=mesh['dp'=8,'expert'=4] {'expert'}, dimensions={0} | all-to-all | bytes 2097152 | tf_op jit(solution)/shard_map/all_to_all | solution.py:206
  607.3 25.1 %multiply_convert_fusion.1 = (bf16[256,5632]{1,0:T(8,128)(2,1)}, bf16[256,5632]{1,0:T(8,128)(2,1)}) fusion(f32[256,11264]{1,0:T(8,128)} %fusion.2, bf16[256,2048]{1,0:T(8,128)(2,1)S(1)} %bitcast.120, bf16[1,5632,2048]{2,1,0:T(8,128)(2,1)} %all-gather.17.cloned.1.call-done), kind=kOutput, calls=%fused_computation.11 | convolution fusion | flops 5924323328 | bytes 41418752 | tf_op jit(solution)/shard_map/dot_general | solution.py:78
  632.4 21.1 %fusion.16 = bf16[256,2048]{1,0:T(8,128)(2,1)} fusion(bf16[1,2048,11264]{2,1,0:T(8,128)(2,1)} %all-gather.15.cloned.1.call-done, bf16[256,5632]{1,0:T(8,128)(2,1)} %get-tuple-element.81, bf16[256,5632]{1,0:T(8,128)(2,1)} %get-tuple-element.80), kind=kOutput, calls=%fused_computation.31 | convolution fusion | flops 11823218688 | bytes 52953088 | tf_op jit(solution)/shard_map/dot_general | solution.py:78
  658.1 24.7 %all-to-all-done.3 = bf16[4,64,2048]{2,1,0:T(8,128)(2,1)} async-done(((bf16[4,64,2048]{2,1,0:T(8,128)(2,1)}), bf16[4,64,2048]{2,1,0:T(8,128)(2,1)}, u32[]{:S(2)}, u32[]{:S(2)}) %all-to-all-start.3) | async-done | bytes 1048608 | tf_op jit(solution)/shard_map/all_to_all | solution.py:229
  689.3 43.7 %all-gather.19.cloned.1.call-done = bf16[512,2048]{1,0:T(8,128)(2,1)} async-done(((bf16[128,2048]{1,0:T(8,128)(2,1)}), bf16[512,2048]{1,0:T(8,128)(2,1)}) %all-gather.19.cloned.1.call-update) | async-done | bytes 2097168 | tf_op jit(solution)/shard_map/all_gather | solution.py:257
  768.9 41.3 %reduce-scatter.14.cloned.1.call-done = bf16[128,2048]{1,0:T(8,128)(2,1)} async-done(((bf16[512,2048]{1,0:T(8,128)(2,1)}), bf16[128,2048]{1,0:T(8,128)(2,1)}) %reduce-scatter.14.cloned.1.call-update) | async-done | bytes 524304 | tf_op jit(solution)/shard_map/reduce_scatter | solution.py:283
  811.7 17.1 all-reduce.4
  830.3 10.1 convolution_bitcast_fusion
  845.5 19.3 %fusion.81 = f32[5632,2048]{1,0:T(8,128)} fusion(bf16[256,5632]{1,0:T(8,128)(2,1)S(1)} %multiply_convert_fusion.2, bf16[256,2048]{1,0:T(8,128)(2,1)} %bitcast.121), kind=kOutput, calls=%fused_computation.154 | convolution fusion | flops 5905580032 | bytes 50069504 | tf_op jit(solution)/shard_map/dot_general | solution.py:72
  866.0 43.8 %fusion.9 = f32[2048,11264]{1,0:T(8,128)} fusion(bf16[256,2048]{1,0:T(8,128)(2,1)S(1)} %bitcast.115, bf16[256,5632]{1,0:T(8,128)(2,1)} %get-tuple-element.81, bf16[256,5632]{1,0:T(8,128)(2,1)} %get-tuple-element.80), kind=kOutput, calls=%fused_computation.23 | convolution fusion | flops 11822694400 | bytes 99090432 | tf_op jit(solution)/shard_map/dot_general | solution.py:72
  911.8 23.0 %all-reduce.3 = (f32[2048]{0:T(1024)S(1)}, f32[2048]{0:T(1024)S(1)}) all-reduce(bf16[2048]{0:T(1024)(128)(2,1)S(1)} %get-tuple-element.71, bf16[2048]{0:T(1024)(128)(2,1)S(1)} %get-tuple-element.72), channel_id=6, replica_groups=mesh['dp'=8,'expert'=4] {'dp'}, use_global_device_ids=true, to_apply=%region_21.22.clone | all-reduce | flops 4096 | bytes 24576
  941.2 19.7 %reduce-scatter.16.cloned.1.call-done = f32[3,256,512]{1,2,0:T(8,128)} async-done(((f32[3,2048,512]{1,2,0:T(8,128)}), f32[3,256,512]{1,2,0:T(8,128)}) %reduce-scatter.16.cloned.1.call-update) | async-done | bytes 1572880 | tf_op jit(solution)/shard_map/reduce_scatter | solution.py:299
  963.9 52.3 %reduce-scatter.18.cloned.1.call-done = f32[512,256]{1,0:T(8,128)} async-done(((f32[512,2048]{1,0:T(8,128)}), f32[512,256]{1,0:T(8,128)}) %reduce-scatter.18.cloned.1.call-update) | async-done | bytes 524304 | tf_op jit(solution)/shard_map/reduce_scatter | solution.py:300
  1016.2 268.8 %reduce-scatter.20.cloned.1.call-done = f32[704,2048]{1,0:T(8,128)} async-done(((f32[5632,2048]{1,0:T(8,128)}), f32[704,2048]{1,0:T(8,128)}) %reduce-scatter.20.cloned.1.call-update) | async-done | bytes 5767184 | tf_op jit(solution)/shard_map/reduce_scatter | solution.py:217
  1285.0 505.4 %reduce-scatter.24.cloned.1.call-done = f32[256,11264]{1,0:T(8,128)} async-done(((f32[2048,11264]{1,0:T(8,128)}), f32[256,11264]{1,0:T(8,128)}) %reduce-scatter.24.cloned.1.call-update) | async-done | bytes 11534352
  (262 shorter events, 169.2 us)
Async XLA Ops:
  7.2 60.7 %all-gather.9.cloned.1.call-start = ((), (), s32[]{:S(2)}) async-start(), calls=%async_computation.11 | async-start | bytes 2621440 | tf_op jit(solution)/shard_map/all_gather | solution.py:126
  8.5 113.6 %copy-start.48 = (f32[128]{0:T(128)}, f32[128]{0:T(128)S(1)}, u32[]{:S(2)}) copy-start(f32[128]{0:T(128)S(1)} %add_rsqrt_fusion.1) | copy-start | bytes 1540
  19.5 102.6 %copy-start.34 = (f32[8,1,256]{2,1,0:T(1,128)}, f32[8,1,256]{2,1,0:T(1,128)S(1)}, u32[]{:S(2)}) copy-start(f32[8,1,256]{2,1,0:T(1,128)S(1)} %convert_element_type.200) | copy-start | bytes 24580
  21.5 94.3 %all-gather.11.cloned.1.call-start = ((), (), s32[]{:S(2)}) async-start(), calls=%async_computation.12 | async-start | bytes 7077888 | tf_op jit(solution)/shard_map/all_gather | solution.py:108
  23.9 122.0 %all-gather.13.cloned.1.call-start = ((), (), s32[]{:S(2)}) async-start(), calls=%async_computation.13 | async-start | bytes 2359296 | tf_op jit(solution)/shard_map/all_gather | solution.py:109
  24.6 169.5 %reduce-scatter.12.cloned.1.call-start = ((), (), s32[]{:S(2)}) async-start(), calls=%async_computation.14 | async-start | bytes 2621440 | tf_op jit(solution)/shard_map/reduce_scatter | solution.py:149
  27.9 103.6 %copy-start.23 = (f32[512,64]{1,0:T(8,128)}, f32[512,64]{1,0:T(8,128)S(1)}, u32[]{:S(2)}) copy-start(f32[512,64]{1,0:T(8,128)S(1)} %get-tuple-element.104) | copy-start | bytes 393220
  150.2 259.9 %all-gather.15.cloned.1.call-start = ((), (), s32[]{:S(2)}) async-start(), calls=%async_computation.15 | async-start | bytes 51904512 | tf_op jit(solution)/shard_map/all_gather | solution.py:65
  150.8 377.8 %all-gather.17.cloned.1.call-start = ((), (), s32[]{:S(2)}) async-start(), calls=%async_computation.16 | async-start | bytes 25952256 | tf_op jit(solution)/shard_map/all_gather | solution.py:66
  160.2 275.7 %copy-start.30 = (f32[8,1,256]{2,1,0:T(1,128)}, f32[8,1,256]{2,1,0:T(1,128)S(1)}, u32[]{:S(2)}) copy-start(f32[8,1,256]{2,1,0:T(1,128)S(1)} %convert_element_type.201) | copy-start | bytes 24580
  162.3 273.6 %copy-start.43 = (s32[128,2]{0,1:T(2,128)}, s32[128,2]{0,1:T(2,128)S(1)}, u32[]{:S(2)}) copy-start(s32[128,2]{0,1:T(2,128)S(1)} %multiply_add_fusion.1) | copy-start | bytes 3076
  195.4 240.5 %copy-start.46 = (f32[128]{0:T(128)}, f32[128]{0:T(128)S(1)}, u32[]{:S(2)}) copy-start(f32[128]{0:T(128)S(1)} %add_rsqrt_fusion) | copy-start | bytes 1540
  196.7 213.4 %copy-start.11 = (bf16[128,2048]{1,0:T(8,128)(2,1)}, bf16[128,2048]{1,0:T(8,128)(2,1)S(1)}, u32[]{:S(2)}) copy-start(bf16[128,2048]{1,0:T(8,128)(2,1)S(1)} %multiply_convert_fusion.7) | copy-start | bytes 1572868
  226.0 184.2 %copy-start.20 = (bf16[4,64,2048]{2,1,0:T(8,128)(2,1)}, bf16[4,64,2048]{2,1,0:T(8,128)(2,1)S(1)}, u32[]{:S(2)}) copy-start(bf16[4,64,2048]{2,1,0:T(8,128)(2,1)S(1)} %all_to_all.20) | copy-start | bytes 3145732
  441.2 104.3 %copy-start.60 = (bf16[256,4]{0,1:T(4,128)(2,1)S(1)}, bf16[256,4]{0,1:T(4,128)(2,1)}, u32[]{:S(2)}) copy-start(bf16[256,4]{0,1:T(4,128)(2,1)} %param.17) | copy-start | bytes 6148
  540.6 30.9 %all-to-all-start.1 = ((bf16[4,64,2048]{2,1,0:T(8,128)(2,1)}), bf16[4,64,2048]{2,1,0:T(8,128)(2,1)}, u32[]{:S(2)}, u32[]{:S(2)}) async-start(bf16[4,64,2048]{2,1,0:T(8,128)(2,1)} %bitcast.129), calls=%async_computation.2 | async-start | bytes 2097152 | tf_op jit(solution)/shard_map/all_to_all | solution.py:177
  653.6 29.2 %all-to-all-start.3 = ((bf16[4,64,2048]{2,1,0:T(8,128)(2,1)}), bf16[4,64,2048]{2,1,0:T(8,128)(2,1)}, u32[]{:S(2)}, u32[]{:S(2)}) async-start(bf16[4,64,2048]{2,1,0:T(8,128)(2,1)} %bitcast.130), calls=%async_computation.4 | async-start | bytes 2097152 | tf_op jit(solution)/shard_map/all_to_all | solution.py:229
  658.0 75.1 %all-gather.19.cloned.1.call-start = ((), (), s32[]{:S(2)}) async-start(), calls=%async_computation.17 | async-start | bytes 2621440 | tf_op jit(solution)/shard_map/all_gather | solution.py:257
  688.8 121.4 %reduce-scatter.14.cloned.1.call-start = ((), (), s32[]{:S(2)}) async-start(), calls=%async_computation.18 | async-start | bytes 2621440 | tf_op jit(solution)/shard_map/reduce_scatter | solution.py:283
  767.5 172.1 %reduce-scatter.22.cloned.1.call-start = ((), (), s32[]{:S(2)}) async-start(), calls=%async_computation.22 | async-start | bytes 1179648
  830.1 130.8 %reduce-scatter.16.cloned.1.call-start = ((), (), s32[]{:S(2)}) async-start(), calls=%async_computation.19 | async-start | bytes 14155776 | tf_op jit(solution)/shard_map/reduce_scatter | solution.py:299
  840.4 175.8 %reduce-scatter.18.cloned.1.call-start = ((), (), s32[]{:S(2)}) async-start(), calls=%async_computation.20 | async-start | bytes 4718592 | tf_op jit(solution)/shard_map/reduce_scatter | solution.py:300
  845.5 439.5 %reduce-scatter.20.cloned.1.call-start = ((), (), s32[]{:S(2)}) async-start(), calls=%async_computation.21 | async-start | bytes 51904512 | tf_op jit(solution)/shard_map/reduce_scatter | solution.py:217
  864.8 925.6 %reduce-scatter.24.cloned.1.call-start = ((), (), s32[]{:S(2)}) async-start(), calls=%async_computation.23 | async-start | bytes 103809024
  (57 other events, 827.3 us)
Sparse Core Ops, SparseCore 0:
  21.7 46.2 all-gather.8
  70.4 45.3 all-gather.10
  117.7 28.1 all-gather.12
  150.2 43.8 reduce-scatter.11
  196.1 214.0 all-gather.14
  412.0 116.4 all-gather.16
  688.9 44.0 all-gather.18
  767.6 42.5 reduce-scatter.13
  830.2 34.4 reduce-scatter.21
  868.0 92.8 reduce-scatter.15
  964.8 51.3 reduce-scatter.17
  1020.7 264.2 reduce-scatter.19
  1289.2 501.1 reduce-scatter.23
where the time goes:
time: 1810 us; the launch traced here: 1800 us
  waiting for transfers between devices  1370 us (76%)
  matrix products  205 us (11%)
  blocking collectives  125 us (7%)
  local copies, waits for them, and re-layouts  41.6 us (2%)
  other arithmetic  33.2 us (2%)
    unnamed x15, waiting for transfers between devices  507 us
    reduce_scatter x1, waiting for transfers between devices, on_device(): lax.psum_scatter(contract_first(columns, d_out_rows), 'dp', scatter_dimen...  269 us
    all_gather x1, waiting for transfers between devices, fetch_expert(): lax.all_gather(w_gate_up, 'dp', axis=1, tiled=True)  184 us
    all_gather x1, waiting for transfers between devices, fetch_expert(): lax.all_gather(w_down, 'dp', axis=1, tiled=True)  87.4 us
    dot_general x6, matrix products, contract_first(): lax.dot_general(left, right, (((0,), (0,)), ((), ())), preferred_element_...  74.2 us
    reduce_scatter x1, waiting for transfers between devices, on_device(): lax.psum_scatter(out_part, 'dp', scatter_dimension=1, tiled=True)  52.3 us
    dot_general x3, matrix products, contract_last(): lax.dot_general(left, right, (((1,), (1,)), ((), ())), preferred_element_...  49.9 us
    all_gather x1, waiting for transfers between devices, on_device(): lax.all_gather(w_qkv, 'dp', axis=1, tiled=True)  47.9 us
  transfers between devices with their start and end apart: 15, of which 14 were waited for; matrix products, arithmetic and copies ran while one was open for 9% of the time, Pallas kernels for 0%

commit v1 on v0

--- a/solution.py
+++ b/solution.py
@@ -9,6 +9,18 @@
 NEGATIVE = -1e30
 THETA = 10000.0
 HIGH = lax.Precision.HIGHEST
+
+
+def gather_by_bits(x, axis, dim):
+    ways, here, lap = (lax.axis_size(axis), lax.axis_index(axis), x.shape[dim])
+    line, have = (x, 1)
+    while have < ways:
+        line = jnp.concatenate(
+            [line, lax.ppermute(line, axis, [(d, (d - have) % ways) for d in range(ways)])],
+            axis=dim,
+        )
+        have = 2 * have
+    return jnp.roll(line, here * lap, axis=dim)
 
 
 def rotary_tables(length_total, head_size):
@@ -62,7 +74,7 @@
 
 def fetch_expert(w_gate_up, w_down):
     gate_up_full, down_full = (
-        lax.all_gather(w_gate_up, "dp", axis=1, tiled=True),
+        gather_by_bits(w_gate_up, "dp", 1),
         lax.all_gather(w_down, "dp", axis=1, tiled=True),
     )
     return (gate_up_full[0], down_full[0])

time: 1810 us -> 2450 us (1.35)
  blocking collectives: 125 us -> 679 us
  other arithmetic: 33.2 us -> 169 us
  waiting for transfers between devices: 1370 us -> 1310 us
    all_gather x1, blocking collectives: 8.85 us -> 593 us  [on_device(): lax.all_gather(gain_ffn, 'dp', axis=0, tiled=True)]
    all_gather x1, waiting for transfers between devices: 7.5 us -> 240 us  [on_device(): lax.all_gather(w_out, 'dp', axis=1, tiled=True)]
    all_gather x1 -> x0, waiting for transfers between devices: 184 us -> none  [fetch_expert(): lax.all_gather(w_gate_up, 'dp', axis=1, tiled=True)]
    squeeze x0 -> x1, other arithmetic: none -> 107 us  [fetch_expert(): return (gate_up_full[0], down_full[0])]
    all_gather x1, waiting for transfers between devices: 87.4 us -> 0.02 us  [fetch_expert(): lax.all_gather(w_down, 'dp', axis=1, tiled=True)]
    ppermute x0 -> x3, waiting for transfers between devices: none -> 71.7 us  [gather_by_bits(): lax.ppermute(line, axis, [(d, (d - have) % ways) for d in range(ways)])]
    all_gather x1, waiting for transfers between devices: 40.1 us -> 0.02 us  [on_device(): whole = lax.all_gather(normalized_input, 'expert', axis=0, tiled=True)]
    reduce_scatter x1, waiting for transfers between devices: 31.7 us -> 0.02 us  [on_device(): lax.psum_scatter(attn_part.astype(jnp.bfloat16), 'expert', scatter_dimens...]
  transfers between devices with their start and end apart: 15 -> 18, of which waited for: 14 -> 11; matrix products, arithmetic and copies ran while one was open for 9% -> 12% of each run, Pallas kernels for 0% -> 0%
where the time goes in v1:
time: 2450 us; the launch traced here: 2440 us
  waiting for transfers between devices  1310 us (53%)
  blocking collectives  679 us (28%)
  matrix products  203 us (8%)
  other arithmetic  169 us (7%)
  local copies, waits for them, and re-layouts  43.4 us (2%)
    all_gather x1, blocking collectives, on_device(): lax.all_gather(gain_ffn, 'dp', axis=0, tiled=True)  593 us
    unnamed x14, waiting for transfers between devices  506 us
    reduce_scatter x1, waiting for transfers between devices, on_device(): lax.psum_scatter(contract_first(columns, d_out_rows), 'dp', scatter_dimen...  269 us
    all_gather x1, waiting for transfers between devices, on_device(): lax.all_gather(w_out, 'dp', axis=1, tiled=True)  240 us
    squeeze x1, other arithmetic, fetch_expert(): return (gate_up_full[0], down_full[0])  107 us
    dot_general x6, matrix products, contract_first(): lax.dot_general(left, right, (((0,), (0,)), ((), ())), preferred_element_...  74.1 us
    ppermute x3, waiting for transfers between devices, gather_by_bits(): lax.ppermute(line, axis, [(d, (d - have) % ways) for d in range(ways)])  71.7 us
    reduce_scatter x1, waiting for transfers between devices, on_device(): lax.psum_scatter(out_part, 'dp', scatter_dimension=1, tiled=True)  52.1 us
  transfers between devices with their start and end apart: 18, of which 11 were waited for; matrix products, arithmetic and copies ran while one was open for 12% of the time, Pallas kernels for 0%

profile of v1, /device:TPU:0, one launch (start us, length us, event | category | flops | bytes accessed | tf_op | source)
XLA Modules:
  0.0 2438.1 jit_solution(13068713858909704740)
XLA Ops:
  7.9 10.3 all-gather
  25.4 71.7 %collective-permute-done = bf16[1,256,11264]{2,1,0:T(8,128)(2,1)S(1)} collective-permute-done((bf16[1,256,11264]{2,1,0:T(8,128)(2,1)}, bf16[1,256,11264]{2,1,0:T(8,128)(2,1)S(1)}, u32[]{:S(2)}, u32[]{:S(2)}) %collective-permute-start) | collective-permute-done | bytes 5767200 | tf_op jit(solution)/shard_map/ppermute | solution.py:19
  109.8 29.6 %all-gather.10.cloned.1.call-done = bf16[3,2048,512]{1,2,0:T(8,128)(2,1)} async-done(((bf16[3,256,512]{1,2,0:T(8,128)(2,1)}), bf16[3,2048,512]{1,2,0:T(8,128)(2,1)}) %all-gather.10.cloned.1.call-update) | async-done | bytes 6291472 | tf_op jit(solution)/shard_map/all_gather | solution.py:120
  161.4 239.9 %all-gather.12.cloned.1.call-done = bf16[512,2048]{1,0:T(8,128)(2,1)} async-done(((bf16[512,256]{1,0:T(8,128)(2,1)}), bf16[512,2048]{1,0:T(8,128)(2,1)}) %all-gather.12.cloned.1.call-update) | async-done | bytes 2097168 | tf_op jit(solution)/shard_map/all_gather | solution.py:121
  406.3 19.8 pad_maximum_fusion
  427.3 593.0 %all-gather.1 = bf16[8,1,256]{2,1,0:T(2,128)(2,1)S(1)} all-gather(bf16[1,1,256]{2,1,0:T(2,128)(2,1)S(1)} %reshape.318), channel_id=1, replica_groups=mesh['dp'=8,'expert'=4] {'dp'}, dimensions={0}, use_global_device_ids=true | all-gather | bytes 4608 | tf_op jit(solution)/shard_map/all_gather | solution.py:123
  1032.3 107.0 %fusion.4 = bf16[2048,11264]{1,0:T(8,128)(2,1)} fusion(s32[]{:T(128)S(6)} %select_n.29, bf16[1,256,11264]{2,1,0:T(8,128)(2,1)} %param.20, bf16[1,256,11264]{2,1,0:T(8,128)(2,1)} %copy-done.2, bf16[1,512,11264]{2,1,0:T(8,128)(2,1)} %collective-permute-done.1, bf16[1,1024,11264]{2,1,0:T(8,128)(2,1)} %collective-permute-done.2), kind=kLoop, calls=%fused_computation.13 | loop fusion | flops 369098752 | bytes 92274688 | tf_op jit(solution)/shard_map/squeeze | solution.py:80
  1140.3 23.0 fusion.83
  1168.5 12.1 fusion.17
  1219.2 27.7 %all_to_all.20 = bf16[4,64,2048]{2,1,0:T(8,128)(2,1)S(1)} all-to-all(bf16[4,64,2048]{2,1,0:T(8,128)(2,1)S(1)} %bitcast.115), channel_id=1, replica_groups=mesh['dp'=8,'expert'=4] {'expert'}, dimensions={0} | all-to-all | bytes 2097152 | tf_op jit(solution)/shard_map/all_to_all | solution.py:218
  1246.9 25.1 %multiply_convert_fusion.1 = (bf16[256,5632]{1,0:T(8,128)(2,1)}, bf16[256,5632]{1,0:T(8,128)(2,1)}) fusion(f32[256,11264]{1,0:T(8,128)} %fusion.83, bf16[256,2048]{1,0:T(8,128)(2,1)S(1)} %bitcast.116, bf16[1,5632,2048]{2,1,0:T(8,128)(2,1)} %all-gather.14.cloned.1.call-done), kind=kOutput, calls=%fused_computation.25 | convolution fusion | flops 5924323328 | bytes 41418752 | tf_op jit(solution)/shard_map/dot_general | solution.py:90
  1272.1 21.1 fusion.21
  1297.7 24.7 %all-to-all-done.3 = bf16[4,64,2048]{2,1,0:T(8,128)(2,1)} async-done(((bf16[4,64,2048]{2,1,0:T(8,128)(2,1)}), bf16[4,64,2048]{2,1,0:T(8,128)(2,1)}, u32[]{:S(2)}, u32[]{:S(2)}) %all-to-all-start.3) | async-done | bytes 1048608 | tf_op jit(solution)/shard_map/all_to_all | solution.py:241
  1329.8 43.7 %all-gather.16.cloned.1.call-done = bf16[512,2048]{1,0:T(8,128)(2,1)} async-done(((bf16[128,2048]{1,0:T(8,128)(2,1)}), bf16[512,2048]{1,0:T(8,128)(2,1)}) %all-gather.16.cloned.1.call-update) | async-done | bytes 2097168 | tf_op jit(solution)/shard_map/all_gather | solution.py:269
  1409.4 41.3 %reduce-scatter.14.cloned.1.call-done = bf16[128,2048]{1,0:T(8,128)(2,1)} async-done(((bf16[512,2048]{1,0:T(8,128)(2,1)}), bf16[128,2048]{1,0:T(8,128)(2,1)}) %reduce-scatter.14.cloned.1.call-update) | async-done | bytes 524304 | tf_op jit(solution)/shard_map/reduce_scatter | solution.py:295
  1452.2 17.1 all-reduce.4
  1470.8 10.1 convolution_bitcast_fusion
  1486.1 19.3 fusion.85
  1506.6 43.8 %fusion.13 = f32[2048,11264]{1,0:T(8,128)} fusion(bf16[256,2048]{1,0:T(8,128)(2,1)S(1)} %bitcast.112, bf16[256,5632]{1,0:T(8,128)(2,1)} %get-tuple-element.82, bf16[256,5632]{1,0:T(8,128)(2,1)} %get-tuple-element.81), kind=kOutput, calls=%fused_computation.37 | convolution fusion | flops 11822694400 | bytes 99090432 | tf_op jit(solution)/shard_map/dot_general | solution.py:84
  1552.3 23.1 all-reduce.3
  1581.8 19.7 reduce-scatter.16.cloned.1.call-done
  1604.5 52.1 %reduce-scatter.18.cloned.1.call-done = f32[512,256]{1,0:T(8,128)} async-done(((f32[512,2048]{1,0:T(8,128)}), f32[512,256]{1,0:T(8,128)}) %reduce-scatter.18.cloned.1.call-update) | async-done | bytes 524304 | tf_op jit(solution)/shard_map/reduce_scatter | solution.py:312
  1656.6 269.0 %reduce-scatter.20.cloned.1.call-done = f32[704,2048]{1,0:T(8,128)} async-done(((f32[5632,2048]{1,0:T(8,128)}), f32[704,2048]{1,0:T(8,128)}) %reduce-scatter.20.cloned.1.call-update) | async-done | bytes 5767184 | tf_op jit(solution)/shard_map/reduce_scatter | solution.py:229
  1925.6 505.2 %reduce-scatter.24.cloned.1.call-done = f32[256,11264]{1,0:T(8,128)} async-done(((f32[2048,11264]{1,0:T(8,128)}), f32[256,11264]{1,0:T(8,128)}) %reduce-scatter.24.cloned.1.call-update) | async-done | bytes 11534352
  (263 shorter events, 171.8 us)
Async XLA Ops:
  7.2 102.6 %all-gather.8.cloned.1.call-start = ((), (), s32[]{:S(2)}) async-start(), calls=%async_computation.11 | async-start | bytes 2621440 | tf_op jit(solution)/shard_map/all_gather | solution.py:138
  18.2 88.1 %copy-start.32 = (f32[8,1,256]{2,1,0:T(1,128)}, f32[8,1,256]{2,1,0:T(1,128)S(1)}, u32[]{:S(2)}) copy-start(f32[8,1,256]{2,1,0:T(1,128)S(1)} %convert_element_type.200) | copy-start | bytes 24580
  19.5 86.9 %copy-start.45 = (f32[128]{0:T(128)}, f32[128]{0:T(128)S(1)}, u32[]{:S(2)}) copy-start(f32[128]{0:T(128)S(1)} %add_rsqrt_fusion.1) | copy-start | bytes 1540
  21.5 117.8 %all-gather.10.cloned.1.call-start = ((), (), s32[]{:S(2)}) async-start(), calls=%async_computation.12 | async-start | bytes 7077888 | tf_op jit(solution)/shard_map/all_gather | solution.py:120
  23.9 377.4 %all-gather.12.cloned.1.call-start = ((), (), s32[]{:S(2)}) async-start(), calls=%async_computation.13 | async-start | bytes 2359296 | tf_op jit(solution)/shard_map/all_gather | solution.py:121
  23.9 73.1 %collective-permute-start = (bf16[1,256,11264]{2,1,0:T(8,128)(2,1)}, bf16[1,256,11264]{2,1,0:T(8,128)(2,1)S(1)}, u32[]{:S(2)}, u32[]{:S(2)}) collective-permute-start(bf16[1,256,11264]{2,1,0:T(8,128)(2,1)} %param.20), channel_id=1, source_target_pairs={{0,28},{4,0},{8,4},{12,8},{16,12},{20,16},{24,20},{28,24},{1,29},{... | collective-permute-start | bytes 17301512 | tf_op jit(solution)/shard_map/ppermute | solution.py:19
  106.4 299.9 %collective-permute-start.1 = (bf16[1,512,11264]{2,1,0:T(8,128)(2,1)}, bf16[1,512,11264]{2,1,0:T(8,128)(2,1)}, u32[]{:S(2)}, u32[]{:S(2)}) collective-permute-start(bf16[1,512,11264]{2,1,0:T(8,128)(2,1)} %pad_maximum_fusion.1), channel_id=1, source_target_pairs={{0,24},{4,28},{8,0},{12,4},{16,8},{20,12},{24,16},{28,20},{1,25},{... | collective-permute-start | bytes 34603016 | tf_op jit(solution)/shard_map/ppermute | solution.py:19
  107.9 914.6 %reduce-scatter.12.cloned.1.call-start = ((), (), s32[]{:S(2)}) async-start(), calls=%async_computation.14 | async-start | bytes 2621440 | tf_op jit(solution)/shard_map/reduce_scatter | solution.py:161
  161.4 264.7 %copy-start.27 = (bf16[4,128,512]{2,1,0:T(8,128)(2,1)}, bf16[4,128,512]{2,1,0:T(8,128)(2,1)S(1)}, u32[]{:S(2)}) copy-start(bf16[4,128,512]{2,1,0:T(8,128)(2,1)S(1)} %fusion.41) | copy-start | bytes 1572868
  405.6 762.9 %all-gather.14.cloned.1.call-start = ((), (), s32[]{:S(2)}) async-start(), calls=%async_computation.15 | async-start | bytes 25952256 | tf_op jit(solution)/shard_map/all_gather | solution.py:78
  406.2 614.0 %copy-start.38 = (s32[128,2]{0,1:T(2,128)S(1)}, s32[128,2]{0,1:T(2,128)}, u32[]{:S(2)}) copy-start(s32[128,2]{0,1:T(2,128)} %param.23) | copy-start | bytes 3076
  406.2 614.3 %copy-start.60 = (s32[128]{0:T(128)S(1)}, s32[128]{0:T(128)}, u32[]{:S(2)}) copy-start(s32[128]{0:T(128)} %param.24) | copy-start | bytes 1540
  406.2 616.4 %copy-start.3 = (bf16[128,2048]{1,0:T(8,128)(2,1)S(1)}, bf16[128,2048]{1,0:T(8,128)(2,1)}, u32[]{:S(2)}) copy-start(bf16[128,2048]{1,0:T(8,128)(2,1)} %param.14) | copy-start | bytes 1572868
  426.1 606.2 %collective-permute-start.2 = (bf16[1,1024,11264]{2,1,0:T(8,128)(2,1)}, bf16[1,1024,11264]{2,1,0:T(8,128)(2,1)}, u32[]{:S(2)}, u32[]{:S(2)}) collective-permute-start(bf16[1,1024,11264]{2,1,0:T(8,128)(2,1)} %pad_maximum_fusion), channel_id=1, source_target_pairs={{0,16},{4,20},{8,24},{12,28},{16,0},{20,4},{24,8},{28,12},{1,17},{... | collective-permute-start | bytes 69206024 | tf_op jit(solution)/shard_map/ppermute | solution.py:19
  1027.4 111.9 %all-to-all-start = ((bf16[4,64,2048]{2,1,0:T(8,128)(2,1)}), bf16[4,64,2048]{2,1,0:T(8,128)(2,1)S(1)}, u32[]{:S(2)}, u32[]{:S(2)}) async-start(bf16[4,64,2048]{2,1,0:T(8,128)(2,1)} %bitcast.13), calls=%async_computation.1 | async-start | bytes 2097152 | tf_op jit(solution)/shard_map/all_to_all | solution.py:176
  1180.6 30.8 %all-to-all-start.1 = ((bf16[4,64,2048]{2,1,0:T(8,128)(2,1)}), bf16[4,64,2048]{2,1,0:T(8,128)(2,1)}, u32[]{:S(2)}, u32[]{:S(2)}) async-start(bf16[4,64,2048]{2,1,0:T(8,128)(2,1)} %bitcast.125), calls=%async_computation.2 | async-start | bytes 2097152 | tf_op jit(solution)/shard_map/all_to_all | solution.py:189
  1293.2 29.2 %all-to-all-start.3 = ((bf16[4,64,2048]{2,1,0:T(8,128)(2,1)}), bf16[4,64,2048]{2,1,0:T(8,128)(2,1)}, u32[]{:S(2)}, u32[]{:S(2)}) async-start(bf16[4,64,2048]{2,1,0:T(8,128)(2,1)} %bitcast.126), calls=%async_computation.4 | async-start | bytes 2097152 | tf_op jit(solution)/shard_map/all_to_all | solution.py:241
  1297.6 75.9 %all-gather.16.cloned.1.call-start = ((), (), s32[]{:S(2)}) async-start(), calls=%async_computation.16 | async-start | bytes 2621440 | tf_op jit(solution)/shard_map/all_gather | solution.py:269
  1329.6 121.2 %reduce-scatter.14.cloned.1.call-start = ((), (), s32[]{:S(2)}) async-start(), calls=%async_computation.17 | async-start | bytes 2621440 | tf_op jit(solution)/shard_map/reduce_scatter | solution.py:295
  1408.0 172.1 %reduce-scatter.22.cloned.1.call-start = ((), (), s32[]{:S(2)}) async-start(), calls=%async_computation.21 | async-start | bytes 1179648
  1470.6 131.0 %reduce-scatter.16.cloned.1.call-start = ((), (), s32[]{:S(2)}) async-start(), calls=%async_computation.18 | async-start | bytes 14155776 | tf_op jit(solution)/shard_map/reduce_scatter | solution.py:311
  1480.9 175.7 %reduce-scatter.18.cloned.1.call-start = ((), (), s32[]{:S(2)}) async-start(), calls=%async_computation.19 | async-start | bytes 4718592 | tf_op jit(solution)/shard_map/reduce_scatter | solution.py:312
  1486.0 439.6 %reduce-scatter.20.cloned.1.call-start = ((), (), s32[]{:S(2)}) async-start(), calls=%async_computation.20 | async-start | bytes 51904512 | tf_op jit(solution)/shard_map/reduce_scatter | solution.py:229
  1505.4 925.5 %reduce-scatter.24.cloned.1.call-start = ((), (), s32[]{:S(2)}) async-start(), calls=%async_computation.22 | async-start | bytes 103809024
  (57 other events, 973.4 us)
Sparse Core Ops, SparseCore 0:
  21.7 46.2 all-gather.7
  70.4 68.9 all-gather.9
  141.2 260.0 all-gather.11
  405.7 43.8 reduce-scatter.11
  451.5 208.7 all-gather.13
  1329.7 43.7 all-gather.15
  1408.1 42.5 reduce-scatter.13
  1470.7 34.3 reduce-scatter.21
  1508.6 92.8 reduce-scatter.15
  1605.3 51.2 reduce-scatter.17
  1661.3 264.3 reduce-scatter.19
  1929.7 501.1 reduce-scatter.23
